TPU v7x, 512 devices: a whole 4x8x8 slice. The times are simulated.
512 devices in a mesh: span: 16 (over z, core), stream: 32 (over x, y).
Axes of the slice: x: 4, y: 8, z: 8, core: 2. Of those that a mesh axis runs over, the one named last changes fastest.
Arguments:
- right_side: float32 [64, 1048576], P(None, ('span', 'stream')), may hold values from -6 to 6
- start_guess: float32 [64, 1048576], P(None, ('span', 'stream')), may hold values from -6 to 6
- fine_matrix: bfloat16 [8192, 5, 128, 128], P(('span', 'stream'))
- fine_columns: int32 [8192, 5], P(('span', 'stream')), may hold values from 0 to 31, as said below
- send_lists: int32 [512, 16], P(('span', 'stream')), may hold values from 0 to 15
- aggregates: int32 [1048576], P(('span', 'stream')), may hold values from 0 to 127
- coarse_matrix: float32 [512, 5, 128, 128], P(('span', 'stream'))
Outputs:
- solution: float32 [64, 1048576], P(None, ('span', 'stream'))
- coarse_correction: float32 [64, 65536], P(None, ('span', 'stream'))
Inputs may be any that keep to these rules, and one draw needn't show every extreme that they name: `fine_columns`: entry 0 of each block row is the row block itself (its local index); the entries of one block row are distinct; entries below 16 name local blocks, entry 16 + d * 4 + h names received slot h from neighbour d; on every device every received slot is named by some block row.
All inputs are finite; a program needn't handle non-finite values.
Results may differ from a plain program's by a relative error of at most 0.0003.
Values sent between devices are 32-bit elements; how exact they have to be, the bound alone decides.
A program may use at most 64 MiB of HBM per device.

v0:
```python
import jax
import jax.numpy as jnp
from jax import lax
from jax.sharding import PartitionSpec as P

center_value = 1.1
radius_value = 0.9
highest = lax.Precision.HIGHEST


def extended_2(block, sides, width):
    for axis, dim in sides:
        count = lax.axis_size(axis)
        forward = [(i, i + 1) for i in range(count - 1)]
        backward = [(target, source) for source, target in forward]
        low = lax.ppermute(
            lax.slice_in_dim(block, block.shape[dim] - width, None, axis=dim), axis, forward
        )
        high = lax.ppermute(lax.slice_in_dim(block, 0, width, axis=dim), axis, backward)
        block = jnp.concatenate([low, block, high], axis=dim)
    return block


def smooth(operator, inverse, target, start):
    if start is None:
        residual = target
        iterate = jnp.zeros_like(target)
    else:
        residual = target - operator(start)
        iterate = start
    update = inverse * residual / center_value
    iterate = iterate + update
    weight_old = radius_value / center_value
    for sweep in range(2):
        residual = residual - operator(update)
        weight_now = 1.0 / (2.0 * center_value / radius_value - weight_old)
        update = (
            weight_now * weight_old * update + 2.0 * weight_now / radius_value * inverse * residual
        )
        iterate = iterate + update
        weight_old = weight_now
    return iterate


def span_rim(to_lower, to_upper):
    stacked = jnp.stack([to_lower, to_upper], 0)
    padded = extended_2(stacked, (("span", 0),), 1)
    return (padded[0], padded[3])


def stream_rim(to_lower, to_upper):
    stacked = jnp.stack([to_lower, to_upper], 0)
    padded = extended_2(stacked, (("stream", 0),), 1)
    return (padded[0], padded[3])


def local(
    right_side, start_guess, fine_matrix, fine_columns, send_lists, aggregates, coarse_matrix
):
    vec_count = right_side.shape[0]
    blk_count = fine_matrix.shape[0]
    nnz_count = fine_matrix.shape[1]
    block_size = fine_matrix.shape[2]
    slot_count = send_lists.shape[1] // 4
    lists = send_lists[0]
    flat_cols = fine_columns.reshape(-1)
    fine_inverse = 1.0 / jnp.diagonal(fine_matrix[:, 0], axis1=1, axis2=2).astype(
        jnp.float32
    ).reshape(-1)

    def receive(blocks):
        sends = jnp.take(blocks, lists, axis=1).reshape(vec_count, 4, slot_count, block_size)
        span_low, span_high = span_rim(sends[:, 0], sends[:, 1])
        stream_low, stream_high = stream_rim(sends[:, 2], sends[:, 3])
        return jnp.concatenate([span_low, span_high, stream_low, stream_high], axis=1)

    def block_product(picked):
        return jnp.einsum(
            "rkij,vrkj->vri", fine_matrix.astype(jnp.float32), picked, precision=highest
        )

    def fine_apply(vector):
        blocks = vector.reshape(vec_count, blk_count, block_size)
        received = receive(blocks)
        extended = jnp.concatenate([blocks, received], axis=1)
        picked = jnp.take(extended, flat_cols, axis=1).reshape(
            vec_count, blk_count, nnz_count, block_size
        )
        return block_product(picked).reshape(vec_count, blk_count * block_size)

    first = smooth(fine_apply, fine_inverse, right_side, start_guess)
    leftover = right_side - fine_apply(first)
    one_hot = (aggregates[:, None] == jnp.arange(block_size, dtype=jnp.int32)[None, :]).astype(
        jnp.float32
    )
    coarse_rhs = jnp.dot(leftover, one_hot, precision=highest)
    coarse_inverse = 1.0 / jnp.diagonal(coarse_matrix[0, 0])

    def coarse_apply(vector):
        span_low, span_high = span_rim(vector, vector)
        stream_low, stream_high = stream_rim(vector, vector)
        extended = jnp.stack([vector, span_low, span_high, stream_low, stream_high], 1)
        return jnp.einsum("kij,vkj->vi", coarse_matrix[0], extended, precision=highest)

    correction = smooth(coarse_apply, coarse_inverse, coarse_rhs, None)
    second = first + jnp.dot(correction, one_hot.T, precision=highest)
    solution = smooth(fine_apply, fine_inverse, right_side, second)
    return (solution, correction)


def solution(mesh):
    placed = (
        P(None, ("span", "stream")),
        P(None, ("span", "stream")),
        P(("span", "stream"), None, None, None),
        P(("span", "stream"), None),
        P(("span", "stream"), None),
        P(("span", "stream")),
        P(("span", "stream"), None, None, None),
    )
    return jax.shard_map(
        local,
        mesh=mesh,
        in_specs=placed,
        out_specs=(P(None, ("span", "stream")), P(None, ("span", "stream"))),
        check_vma=False,
    )
```

profile of v0, /device:TPU:251, one launch (start us, length us, event | category | flops | bytes accessed | tf_op | source)
XLA Modules:
  0.0 281.2 jit_solution(12798874371260927000)
XLA Ops:
  7.6 4.4 %collective-permute-start.2 = (f32[1,64,4,128]{3,1,2,0:T(8,128)S(1)}, f32[1,64,4,128]{3,1,2,0:T(8,128)S(1)}, u32[]{:S(2)}, u32[]{:S(2)}) collective-permute-start(f32[1,64,4,128]{3,1,2,0:T(8,128)S(1)} %get-tuple-element.31), channel_id=1, source_target_pairs={{0,1},{1,2},{2,3},{3,4},{4,5},{5,6},{6,7},{7,8},{8,9},{9,10},{10,1... | collective-permute-start | bytes 393224 | tf_op jit(solution)/shard_map/ppermute | solution.py:16
  15.1 5.1 %collective-permute-start = (f32[1,64,4,128]{3,1,2,0:T(8,128)}, f32[1,64,4,128]{3,1,2,0:T(8,128)S(1)}, u32[]{:S(2)}, u32[]{:S(2)}) collective-permute-start(f32[1,64,4,128]{3,1,2,0:T(8,128)} %get-tuple-element.33), channel_id=1, source_target_pairs={{0,32},{32,64},{64,96},{96,128},{128,160},{160,192},{192,224},{224... | collective-permute-start | bytes 393224 | tf_op jit(solution)/shard_map/ppermute | solution.py:16
  31.9 3.3 %convolution_bitcast_fusion.6 = f32[16,8,8,128]{3,2,1,0:T(8,128)S(1)} fusion(f32[64,16,5,128]{3,0,2,1:T(8,128)S(1)} %bitcast.383, bf16[16,5,128,128]{3,2,1,0:T(8,128)(2,1)S(1)} %copy-done), kind=kOutput, calls=%fused_computation.30 | convolution fusion | flops 1006632960 | bytes 5767168 | tf_op jit(solution)/shard_map/rkij,vrkj->vri/dot_general | solution.py:78
  46.7 5.5 %collective-permute-start.6 = (f32[1,64,4,128]{3,1,2,0:T(8,128)S(1)}, f32[1,64,4,128]{3,1,2,0:T(8,128)S(1)}, u32[]{:S(2)}, u32[]{:S(2)}) collective-permute-start(f32[1,64,4,128]{3,1,2,0:T(8,128)S(1)} %get-tuple-element.27), channel_id=1, source_target_pairs={{0,1},{1,2},{2,3},{3,4},{4,5},{5,6},{6,7},{7,8},{8,9},{9,10},{10,1... | collective-permute-start | bytes 393224 | tf_op jit(solution)/shard_map/ppermute | solution.py:16
  55.3 4.4 %collective-permute-done.5 = f32[1,64,4,128]{3,1,2,0:T(8,128)S(1)} collective-permute-done((f32[1,64,4,128]{3,1,2,0:T(8,128)S(1)}, f32[1,64,4,128]{3,1,2,0:T(8,128)S(1)}, u32[]{:S(2)}, u32[]{:S(2)}) %collective-permute-start.5) | collective-permute-done | bytes 131104 | tf_op jit(solution)/shard_map/ppermute | solution.py:19
  61.7 3.4 %gather_fusion.5 = f32[80,64,128]{2,1,0:T(8,128)} fusion(f32[64,32,128]{2,0,1:T(8,128)} %bitcast_dynamic-update-slice_fusion.20, s32[1024]{0:T(1024)S(1)} %pad_clamp_fusion), kind=kCustom, calls=%fused_computation.8.clone | custom fusion | bytes 5243200 | tf_op jit(solution)/shard_map/jit(_take)/gather | solution.py:86
  67.1 3.3 %convolution_bitcast_fusion.5 = f32[16,8,8,128]{3,2,1,0:T(8,128)S(1)} fusion(f32[64,16,5,128]{3,0,2,1:T(8,128)S(1)} %bitcast.384, bf16[16,5,128,128]{3,2,1,0:T(8,128)(2,1)S(1)} %copy-done), kind=kOutput, calls=%fused_computation.29 | convolution fusion | flops 1006632960 | bytes 5767168 | tf_op jit(solution)/shard_map/rkij,vrkj->vri/dot_general | solution.py:78
  77.8 5.5 %collective-permute-start.10 = (f32[1,64,4,128]{3,1,2,0:T(8,128)S(1)}, f32[1,64,4,128]{3,1,2,0:T(8,128)S(1)}, u32[]{:S(2)}, u32[]{:S(2)}) collective-permute-start(f32[1,64,4,128]{3,1,2,0:T(8,128)S(1)} %get-tuple-element.23), channel_id=1, source_target_pairs={{0,1},{1,2},{2,3},{3,4},{4,5},{5,6},{6,7},{7,8},{8,9},{9,10},{10,1... | collective-permute-start | bytes 393224 | tf_op jit(solution)/shard_map/ppermute | solution.py:16
  85.2 5.0 %collective-permute-start.8 = (f32[1,64,4,128]{3,1,2,0:T(8,128)S(1)}, f32[1,64,4,128]{3,1,2,0:T(8,128)S(1)}, u32[]{:S(2)}, u32[]{:S(2)}) collective-permute-start(f32[1,64,4,128]{3,1,2,0:T(8,128)S(1)} %get-tuple-element.25), channel_id=1, source_target_pairs={{0,32},{32,64},{64,96},{96,128},{128,160},{160,192},{192,224},{224... | collective-permute-start | bytes 393224 | tf_op jit(solution)/shard_map/ppermute | solution.py:16
  94.8 3.4 %gather_fusion.7 = f32[80,64,128]{2,1,0:T(8,128)} fusion(f32[64,32,128]{2,0,1:T(8,128)} %bitcast_dynamic-update-slice_fusion.16, s32[1024]{0:T(1024)S(1)} %pad_clamp_fusion), kind=kCustom, calls=%fused_computation.9.clone | custom fusion | bytes 5243200 | tf_op jit(solution)/shard_map/jit(_take)/gather | solution.py:86
  100.2 3.3 %convolution_bitcast_fusion.4 = f32[16,8,8,128]{3,2,1,0:T(8,128)S(1)} fusion(f32[64,16,5,128]{3,0,2,1:T(8,128)S(1)} %bitcast.385, bf16[16,5,128,128]{3,2,1,0:T(8,128)(2,1)S(1)} %copy-done), kind=kOutput, calls=%fused_computation.28 | convolution fusion | flops 1006632960 | bytes 5767168 | tf_op jit(solution)/shard_map/rkij,vrkj->vri/dot_general | solution.py:78
  111.0 5.5 %collective-permute-start.14 = (f32[1,64,4,128]{3,1,2,0:T(8,128)S(1)}, f32[1,64,4,128]{3,1,2,0:T(8,128)S(1)}, u32[]{:S(2)}, u32[]{:S(2)}) collective-permute-start(f32[1,64,4,128]{3,1,2,0:T(8,128)S(1)} %get-tuple-element.19), channel_id=1, source_target_pairs={{0,1},{1,2},{2,3},{3,4},{4,5},{5,6},{6,7},{7,8},{8,9},{9,10},{10,1... | collective-permute-start | bytes 393224 | tf_op jit(solution)/shard_map/ppermute | solution.py:16
  118.4 6.0 %collective-permute-start.12 = (f32[1,64,4,128]{3,1,2,0:T(8,128)S(1)}, f32[1,64,4,128]{3,1,2,0:T(8,128)S(1)}, u32[]{:S(2)}, u32[]{:S(2)}) collective-permute-start(f32[1,64,4,128]{3,1,2,0:T(8,128)S(1)} %get-tuple-element.21), channel_id=1, source_target_pairs={{0,32},{32,64},{64,96},{96,128},{128,160},{160,192},{192,224},{224... | collective-permute-start | bytes 393224 | tf_op jit(solution)/shard_map/ppermute | solution.py:16
  129.0 3.4 %gather_fusion.9 = f32[80,64,128]{2,1,0:T(8,128)} fusion(f32[64,32,128]{2,0,1:T(8,128)} %bitcast_dynamic-update-slice_fusion.12, s32[1024]{0:T(1024)S(1)} %pad_clamp_fusion), kind=kCustom, calls=%fused_computation.10.clone | custom fusion | bytes 5243200 | tf_op jit(solution)/shard_map/jit(_take)/gather | solution.py:86
  134.4 3.3 %convolution_bitcast_fusion.3 = f32[16,8,8,128]{3,2,1,0:T(8,128)S(1)} fusion(f32[64,16,5,128]{3,0,2,1:T(8,128)S(1)} %bitcast.386, bf16[16,5,128,128]{3,2,1,0:T(8,128)(2,1)S(1)} %copy-done), kind=kOutput, calls=%fused_computation.27 | convolution fusion | flops 1006632960 | bytes 5767168 | tf_op jit(solution)/shard_map/rkij,vrkj->vri/dot_general | solution.py:78
  138.3 5.6 %collective-permute-start.16 = (f32[1,64,128]{2,1,0:T(8,128)S(1)}, f32[1,64,128]{2,1,0:T(8,128)S(1)}, u32[]{:S(2)}, u32[]{:S(2)}) collective-permute-start(f32[1,64,128]{2,1,0:T(8,128)S(1)} %fusion.19), channel_id=1, source_target_pairs={{0,32},{32,64},{64,96},{96,128},{128,160},{160,192},{192,224},{224... | collective-permute-start | bytes 98312 | tf_op jit(solution)/shard_map/ppermute | solution.py:16
  145.9 5.5 %collective-permute-start.18 = (f32[1,64,128]{2,1,0:T(8,128)S(1)}, f32[1,64,128]{2,1,0:T(8,128)S(1)}, u32[]{:S(2)}, u32[]{:S(2)}) collective-permute-start(f32[1,64,128]{2,1,0:T(8,128)S(1)} %fusion.19), channel_id=1, source_target_pairs={{0,1},{1,2},{2,3},{3,4},{4,5},{5,6},{6,7},{7,8},{8,9},{9,10},{10,1... | collective-permute-start | bytes 98312 | tf_op jit(solution)/shard_map/ppermute | solution.py:16
  153.3 4.5 %collective-permute-done.17 = f32[1,64,128]{2,1,0:T(8,128)S(1)} collective-permute-done((f32[1,64,128]{2,1,0:T(8,128)S(1)}, f32[1,64,128]{2,1,0:T(8,128)S(1)}, u32[]{:S(2)}, u32[]{:S(2)}) %collective-permute-start.17) | collective-permute-done | bytes 32800 | tf_op jit(solution)/shard_map/ppermute | solution.py:19
  162.2 5.5 %collective-permute-start.22 = (f32[1,64,128]{2,1,0:T(8,128)S(1)}, f32[1,64,128]{2,1,0:T(8,128)S(1)}, u32[]{:S(2)}, u32[]{:S(2)}) collective-permute-start(f32[1,64,128]{2,1,0:T(8,128)S(1)} %fusion.20), channel_id=1, source_target_pairs={{0,1},{1,2},{2,3},{3,4},{4,5},{5,6},{6,7},{7,8},{8,9},{9,10},{10,1... | collective-permute-start | bytes 98312 | tf_op jit(solution)/shard_map/ppermute | solution.py:16
  170.7 3.4 %collective-permute-done.21 = f32[1,64,128]{2,1,0:T(8,128)S(1)} collective-permute-done((f32[1,64,128]{2,1,0:T(8,128)S(1)}, f32[1,64,128]{2,1,0:T(8,128)S(1)}, u32[]{:S(2)}, u32[]{:S(2)}) %collective-permute-start.21) | collective-permute-done | bytes 32800 | tf_op jit(solution)/shard_map/ppermute | solution.py:19
  183.0 5.5 %collective-permute-start.26 = (f32[1,64,4,128]{3,1,2,0:T(8,128)S(1)}, f32[1,64,4,128]{3,1,2,0:T(8,128)S(1)}, u32[]{:S(2)}, u32[]{:S(2)}) collective-permute-start(f32[1,64,4,128]{3,1,2,0:T(8,128)S(1)} %get-tuple-element.15), channel_id=1, source_target_pairs={{0,1},{1,2},{2,3},{3,4},{4,5},{5,6},{6,7},{7,8},{8,9},{9,10},{10,1... | collective-permute-start | bytes 393224 | tf_op jit(solution)/shard_map/ppermute | solution.py:16
  190.4 4.9 %collective-permute-start.24 = (f32[1,64,4,128]{3,1,2,0:T(8,128)S(1)}, f32[1,64,4,128]{3,1,2,0:T(8,128)S(1)}, u32[]{:S(2)}, u32[]{:S(2)}) collective-permute-start(f32[1,64,4,128]{3,1,2,0:T(8,128)S(1)} %get-tuple-element.17), channel_id=1, source_target_pairs={{0,32},{32,64},{64,96},{96,128},{128,160},{160,192},{192,224},{224... | collective-permute-start | bytes 393224 | tf_op jit(solution)/shard_map/ppermute | solution.py:16
  199.9 3.4 %gather_fusion.11 = f32[80,64,128]{2,1,0:T(8,128)} fusion(f32[64,32,128]{2,0,1:T(8,128)} %bitcast_dynamic-update-slice_fusion.8, s32[1024]{0:T(1024)S(1)} %pad_clamp_fusion), kind=kCustom, calls=%fused_computation.11.clone | custom fusion | bytes 5243200 | tf_op jit(solution)/shard_map/jit(_take)/gather | solution.py:86
  213.9 5.8 %collective-permute-start.28 = (f32[1,64,4,128]{3,1,2,0:T(8,128)S(1)}, f32[1,64,4,128]{3,1,2,0:T(8,128)S(1)}, u32[]{:S(2)}, u32[]{:S(2)}) collective-permute-start(f32[1,64,4,128]{3,1,2,0:T(8,128)S(1)} %get-tuple-element.13), channel_id=1, source_target_pairs={{0,32},{32,64},{64,96},{96,128},{128,160},{160,192},{192,224},{224... | collective-permute-start | bytes 393224 | tf_op jit(solution)/shard_map/ppermute | solution.py:16
  223.5 5.5 %collective-permute-start.30 = (f32[1,64,4,128]{3,1,2,0:T(8,128)S(1)}, f32[1,64,4,128]{3,1,2,0:T(8,128)S(1)}, u32[]{:S(2)}, u32[]{:S(2)}) collective-permute-start(f32[1,64,4,128]{3,1,2,0:T(8,128)S(1)} %get-tuple-element.11), channel_id=1, source_target_pairs={{0,1},{1,2},{2,3},{3,4},{4,5},{5,6},{6,7},{7,8},{8,9},{9,10},{10,1... | collective-permute-start | bytes 393224 | tf_op jit(solution)/shard_map/ppermute | solution.py:16
  231.6 4.9 %collective-permute-done.29 = f32[1,64,4,128]{3,1,2,0:T(8,128)S(1)} collective-permute-done((f32[1,64,4,128]{3,1,2,0:T(8,128)S(1)}, f32[1,64,4,128]{3,1,2,0:T(8,128)S(1)}, u32[]{:S(2)}, u32[]{:S(2)}) %collective-permute-start.29) | collective-permute-done | bytes 131104 | tf_op jit(solution)/shard_map/ppermute | solution.py:19
  238.5 3.4 %gather_fusion.13 = f32[80,64,128]{2,1,0:T(8,128)} fusion(f32[64,32,128]{2,0,1:T(8,128)} %bitcast_dynamic-update-slice_fusion.4, s32[1024]{0:T(1024)S(1)} %pad_clamp_fusion), kind=kCustom, calls=%fused_computation.12.clone | custom fusion | bytes 5243200 | tf_op jit(solution)/shard_map/jit(_take)/gather | solution.py:86
  243.9 3.3 %convolution_bitcast_fusion.1 = f32[16,8,8,128]{3,2,1,0:T(8,128)S(1)} fusion(f32[64,16,5,128]{3,0,2,1:T(8,128)S(1)} %bitcast.388, bf16[16,5,128,128]{3,2,1,0:T(8,128)(2,1)S(1)} %copy-done), kind=kOutput, calls=%fused_computation.25 | convolution fusion | flops 1006632960 | bytes 5767168 | tf_op jit(solution)/shard_map/rkij,vrkj->vri/dot_general | solution.py:78
  254.5 5.5 %collective-permute-start.34 = (f32[1,64,4,128]{3,1,2,0:T(8,128)S(1)}, f32[1,64,4,128]{3,1,2,0:T(8,128)S(1)}, u32[]{:S(2)}, u32[]{:S(2)}) collective-permute-start(f32[1,64,4,128]{3,1,2,0:T(8,128)S(1)} %get-tuple-element.7), channel_id=1, source_target_pairs={{0,1},{1,2},{2,3},{3,4},{4,5},{5,6},{6,7},{7,8},{8,9},{9,10},{10,1... | collective-permute-start | bytes 393224 | tf_op jit(solution)/shard_map/ppermute | solution.py:16
  262.0 4.9 %collective-permute-start.32 = (f32[1,64,4,128]{3,1,2,0:T(8,128)S(1)}, f32[1,64,4,128]{3,1,2,0:T(8,128)S(1)}, u32[]{:S(2)}, u32[]{:S(2)}) collective-permute-start(f32[1,64,4,128]{3,1,2,0:T(8,128)S(1)} %get-tuple-element.9), channel_id=1, source_target_pairs={{0,32},{32,64},{64,96},{96,128},{128,160},{160,192},{192,224},{224... | collective-permute-start | bytes 393224 | tf_op jit(solution)/shard_map/ppermute | solution.py:16
  271.4 3.4 %gather_fusion.15 = f32[80,64,128]{2,1,0:T(8,128)} fusion(f32[64,32,128]{2,0,1:T(8,128)} %bitcast_dynamic-update-slice_fusion, s32[1024]{0:T(1024)S(1)} %pad_clamp_fusion), kind=kCustom, calls=%fused_computation.13.clone | custom fusion | bytes 5243200 | tf_op jit(solution)/shard_map/jit(_take)/gather | solution.py:86
  276.9 3.3 %convolution_bitcast_fusion = f32[16,8,8,128]{3,2,1,0:T(8,128)S(1)} fusion(f32[64,16,5,128]{3,0,2,1:T(8,128)S(1)} %bitcast.382, bf16[16,5,128,128]{3,2,1,0:T(8,128)(2,1)S(1)} %copy-done), kind=kOutput, calls=%fused_computation.24 | convolution fusion | flops 1006632960 | bytes 5767168 | tf_op jit(solution)/shard_map/rkij,vrkj->vri/dot_general | solution.py:78
  (210 shorter events, 136.9 us)
Async XLA Ops:
  4.6 22.6 %collective-permute-start.3 = (f32[1,64,4,128]{3,1,2,0:T(8,128)S(1)}, f32[1,64,4,128]{3,1,2,0:T(8,128)S(1)}, u32[]{:S(2)}, u32[]{:S(2)}) collective-permute-start(f32[1,64,4,128]{3,1,2,0:T(8,128)S(1)} %get-tuple-element.30), channel_id=1, source_target_pairs={{1,0},{2,1},{3,2},{4,3},{5,4},{6,5},{7,6},{8,7},{9,8},{10,9},{11,1... | collective-permute-start | bytes 393224 | tf_op jit(solution)/shard_map/ppermute | solution.py:19
  7.6 19.6 %collective-permute-start.2 = (f32[1,64,4,128]{3,1,2,0:T(8,128)S(1)}, f32[1,64,4,128]{3,1,2,0:T(8,128)S(1)}, u32[]{:S(2)}, u32[]{:S(2)}) collective-permute-start(f32[1,64,4,128]{3,1,2,0:T(8,128)S(1)} %get-tuple-element.31), channel_id=1, source_target_pairs={{0,1},{1,2},{2,3},{3,4},{4,5},{5,6},{6,7},{7,8},{8,9},{9,10},{10,1... | collective-permute-start | bytes 393224 | tf_op jit(solution)/shard_map/ppermute | solution.py:16
  12.0 15.1 %collective-permute-start.1 = (f32[1,64,4,128]{3,1,2,0:T(8,128)S(1)}, f32[1,64,4,128]{3,1,2,0:T(8,128)S(1)}, u32[]{:S(2)}, u32[]{:S(2)}) collective-permute-start(f32[1,64,4,128]{3,1,2,0:T(8,128)S(1)} %get-tuple-element.32), channel_id=1, source_target_pairs={{32,0},{64,32},{96,64},{128,96},{160,128},{192,160},{224,192},{256... | collective-permute-start | bytes 393224 | tf_op jit(solution)/shard_map/ppermute | solution.py:19
  15.1 11.9 %collective-permute-start = (f32[1,64,4,128]{3,1,2,0:T(8,128)}, f32[1,64,4,128]{3,1,2,0:T(8,128)S(1)}, u32[]{:S(2)}, u32[]{:S(2)}) collective-permute-start(f32[1,64,4,128]{3,1,2,0:T(8,128)} %get-tuple-element.33), channel_id=1, source_target_pairs={{0,32},{32,64},{64,96},{96,128},{128,160},{160,192},{192,224},{224... | collective-permute-start | bytes 393224 | tf_op jit(solution)/shard_map/ppermute | solution.py:16
  40.5 14.2 %collective-permute-start.4 = (f32[1,64,4,128]{3,1,2,0:T(8,128)S(1)}, f32[1,64,4,128]{3,1,2,0:T(8,128)S(1)}, u32[]{:S(2)}, u32[]{:S(2)}) collective-permute-start(f32[1,64,4,128]{3,1,2,0:T(8,128)S(1)} %get-tuple-element.29), channel_id=1, source_target_pairs={{0,32},{32,64},{64,96},{96,128},{128,160},{160,192},{192,224},{224... | collective-permute-start | bytes 393224 | tf_op jit(solution)/shard_map/ppermute | solution.py:16
  44.8 16.2 %collective-permute-start.7 = (f32[1,64,4,128]{3,1,2,0:T(8,128)S(1)}, f32[1,64,4,128]{3,1,2,0:T(8,128)S(1)}, u32[]{:S(2)}, u32[]{:S(2)}) collective-permute-start(f32[1,64,4,128]{3,1,2,0:T(8,128)S(1)} %get-tuple-element.26), channel_id=1, source_target_pairs={{1,0},{2,1},{3,2},{4,3},{5,4},{6,5},{7,6},{8,7},{9,8},{10,9},{11,1... | collective-permute-start | bytes 393224 | tf_op jit(solution)/shard_map/ppermute | solution.py:19
  46.7 13.6 %collective-permute-start.6 = (f32[1,64,4,128]{3,1,2,0:T(8,128)S(1)}, f32[1,64,4,128]{3,1,2,0:T(8,128)S(1)}, u32[]{:S(2)}, u32[]{:S(2)}) collective-permute-start(f32[1,64,4,128]{3,1,2,0:T(8,128)S(1)} %get-tuple-element.27), channel_id=1, source_target_pairs={{0,1},{1,2},{2,3},{3,4},{4,5},{5,6},{6,7},{7,8},{8,9},{9,10},{10,1... | collective-permute-start | bytes 393224 | tf_op jit(solution)/shard_map/ppermute | solution.py:16
  52.2 7.5 %collective-permute-start.5 = (f32[1,64,4,128]{3,1,2,0:T(8,128)S(1)}, f32[1,64,4,128]{3,1,2,0:T(8,128)S(1)}, u32[]{:S(2)}, u32[]{:S(2)}) collective-permute-start(f32[1,64,4,128]{3,1,2,0:T(8,128)S(1)} %get-tuple-element.28), channel_id=1, source_target_pairs={{32,0},{64,32},{96,64},{128,96},{160,128},{192,160},{224,192},{256... | collective-permute-start | bytes 393224 | tf_op jit(solution)/shard_map/ppermute | solution.py:19
  75.9 18.3 %collective-permute-start.11 = (f32[1,64,4,128]{3,1,2,0:T(8,128)S(1)}, f32[1,64,4,128]{3,1,2,0:T(8,128)S(1)}, u32[]{:S(2)}, u32[]{:S(2)}) collective-permute-start(f32[1,64,4,128]{3,1,2,0:T(8,128)S(1)} %get-tuple-element.22), channel_id=1, source_target_pairs={{1,0},{2,1},{3,2},{4,3},{5,4},{6,5},{7,6},{8,7},{9,8},{10,9},{11,1... | collective-permute-start | bytes 393224 | tf_op jit(solution)/shard_map/ppermute | solution.py:19
  77.8 15.7 %collective-permute-start.10 = (f32[1,64,4,128]{3,1,2,0:T(8,128)S(1)}, f32[1,64,4,128]{3,1,2,0:T(8,128)S(1)}, u32[]{:S(2)}, u32[]{:S(2)}) collective-permute-start(f32[1,64,4,128]{3,1,2,0:T(8,128)S(1)} %get-tuple-element.23), channel_id=1, source_target_pairs={{0,1},{1,2},{2,3},{3,4},{4,5},{5,6},{6,7},{7,8},{8,9},{9,10},{10,1... | collective-permute-start | bytes 393224 | tf_op jit(solution)/shard_map/ppermute | solution.py:16
  83.3 9.5 %collective-permute-start.9 = (f32[1,64,4,128]{3,1,2,0:T(8,128)S(1)}, f32[1,64,4,128]{3,1,2,0:T(8,128)S(1)}, u32[]{:S(2)}, u32[]{:S(2)}) collective-permute-start(f32[1,64,4,128]{3,1,2,0:T(8,128)S(1)} %get-tuple-element.24), channel_id=1, source_target_pairs={{32,0},{64,32},{96,64},{128,96},{160,128},{192,160},{224,192},{256... | collective-permute-start | bytes 393224 | tf_op jit(solution)/shard_map/ppermute | solution.py:19
  85.2 6.9 %collective-permute-start.8 = (f32[1,64,4,128]{3,1,2,0:T(8,128)S(1)}, f32[1,64,4,128]{3,1,2,0:T(8,128)S(1)}, u32[]{:S(2)}, u32[]{:S(2)}) collective-permute-start(f32[1,64,4,128]{3,1,2,0:T(8,128)S(1)} %get-tuple-element.25), channel_id=1, source_target_pairs={{0,32},{32,64},{64,96},{96,128},{128,160},{160,192},{192,224},{224... | collective-permute-start | bytes 393224 | tf_op jit(solution)/shard_map/ppermute | solution.py:16
  109.1 19.3 %collective-permute-start.15 = (f32[1,64,4,128]{3,1,2,0:T(8,128)S(1)}, f32[1,64,4,128]{3,1,2,0:T(8,128)S(1)}, u32[]{:S(2)}, u32[]{:S(2)}) collective-permute-start(f32[1,64,4,128]{3,1,2,0:T(8,128)S(1)} %get-tuple-element.18), channel_id=1, source_target_pairs={{1,0},{2,1},{3,2},{4,3},{5,4},{6,5},{7,6},{8,7},{9,8},{10,9},{11,1... | collective-permute-start | bytes 393224 | tf_op jit(solution)/shard_map/ppermute | solution.py:19
  111.0 16.7 %collective-permute-start.14 = (f32[1,64,4,128]{3,1,2,0:T(8,128)S(1)}, f32[1,64,4,128]{3,1,2,0:T(8,128)S(1)}, u32[]{:S(2)}, u32[]{:S(2)}) collective-permute-start(f32[1,64,4,128]{3,1,2,0:T(8,128)S(1)} %get-tuple-element.19), channel_id=1, source_target_pairs={{0,1},{1,2},{2,3},{3,4},{4,5},{5,6},{6,7},{7,8},{8,9},{9,10},{10,1... | collective-permute-start | bytes 393224 | tf_op jit(solution)/shard_map/ppermute | solution.py:16
  116.5 10.5 %collective-permute-start.13 = (f32[1,64,4,128]{3,1,2,0:T(8,128)S(1)}, f32[1,64,4,128]{3,1,2,0:T(8,128)S(1)}, u32[]{:S(2)}, u32[]{:S(2)}) collective-permute-start(f32[1,64,4,128]{3,1,2,0:T(8,128)S(1)} %get-tuple-element.20), channel_id=1, source_target_pairs={{32,0},{64,32},{96,64},{128,96},{160,128},{192,160},{224,192},{256... | collective-permute-start | bytes 393224 | tf_op jit(solution)/shard_map/ppermute | solution.py:19
  118.4 7.9 %collective-permute-start.12 = (f32[1,64,4,128]{3,1,2,0:T(8,128)S(1)}, f32[1,64,4,128]{3,1,2,0:T(8,128)S(1)}, u32[]{:S(2)}, u32[]{:S(2)}) collective-permute-start(f32[1,64,4,128]{3,1,2,0:T(8,128)S(1)} %get-tuple-element.21), channel_id=1, source_target_pairs={{0,32},{32,64},{64,96},{96,128},{128,160},{160,192},{192,224},{224... | collective-permute-start | bytes 393224 | tf_op jit(solution)/shard_map/ppermute | solution.py:16
  138.3 14.9 %collective-permute-start.16 = (f32[1,64,128]{2,1,0:T(8,128)S(1)}, f32[1,64,128]{2,1,0:T(8,128)S(1)}, u32[]{:S(2)}, u32[]{:S(2)}) collective-permute-start(f32[1,64,128]{2,1,0:T(8,128)S(1)} %fusion.19), channel_id=1, source_target_pairs={{0,32},{32,64},{64,96},{96,128},{128,160},{160,192},{192,224},{224... | collective-permute-start | bytes 98312 | tf_op jit(solution)/shard_map/ppermute | solution.py:16
  143.9 13.9 %collective-permute-start.19 = (f32[1,64,128]{2,1,0:T(8,128)S(1)}, f32[1,64,128]{2,1,0:T(8,128)S(1)}, u32[]{:S(2)}, u32[]{:S(2)}) collective-permute-start(f32[1,64,128]{2,1,0:T(8,128)S(1)} %fusion.19), channel_id=1, source_target_pairs={{1,0},{2,1},{3,2},{4,3},{5,4},{6,5},{7,6},{8,7},{9,8},{10,9},{11,1... | collective-permute-start | bytes 98312 | tf_op jit(solution)/shard_map/ppermute | solution.py:19
  145.9 11.9 %collective-permute-start.18 = (f32[1,64,128]{2,1,0:T(8,128)S(1)}, f32[1,64,128]{2,1,0:T(8,128)S(1)}, u32[]{:S(2)}, u32[]{:S(2)}) collective-permute-start(f32[1,64,128]{2,1,0:T(8,128)S(1)} %fusion.19), channel_id=1, source_target_pairs={{0,1},{1,2},{2,3},{3,4},{4,5},{5,6},{6,7},{7,8},{8,9},{9,10},{10,1... | collective-permute-start | bytes 98312 | tf_op jit(solution)/shard_map/ppermute | solution.py:16
  158.4 12.3 %collective-permute-start.20 = (f32[1,64,128]{2,1,0:T(8,128)S(1)}, f32[1,64,128]{2,1,0:T(8,128)S(1)}, u32[]{:S(2)}, u32[]{:S(2)}) collective-permute-start(f32[1,64,128]{2,1,0:T(8,128)S(1)} %fusion.20), channel_id=1, source_target_pairs={{0,32},{32,64},{64,96},{96,128},{128,160},{160,192},{192,224},{224... | collective-permute-start | bytes 98312 | tf_op jit(solution)/shard_map/ppermute | solution.py:16
  160.3 13.9 %collective-permute-start.23 = (f32[1,64,128]{2,1,0:T(8,128)S(1)}, f32[1,64,128]{2,1,0:T(8,128)S(1)}, u32[]{:S(2)}, u32[]{:S(2)}) collective-permute-start(f32[1,64,128]{2,1,0:T(8,128)S(1)} %fusion.20), channel_id=1, source_target_pairs={{1,0},{2,1},{3,2},{4,3},{5,4},{6,5},{7,6},{8,7},{9,8},{10,9},{11,1... | collective-permute-start | bytes 98312 | tf_op jit(solution)/shard_map/ppermute | solution.py:19
  162.2 11.9 %collective-permute-start.22 = (f32[1,64,128]{2,1,0:T(8,128)S(1)}, f32[1,64,128]{2,1,0:T(8,128)S(1)}, u32[]{:S(2)}, u32[]{:S(2)}) collective-permute-start(f32[1,64,128]{2,1,0:T(8,128)S(1)} %fusion.20), channel_id=1, source_target_pairs={{0,1},{1,2},{2,3},{3,4},{4,5},{5,6},{6,7},{7,8},{8,9},{9,10},{10,1... | collective-permute-start | bytes 98312 | tf_op jit(solution)/shard_map/ppermute | solution.py:16
  181.1 18.1 %collective-permute-start.27 = (f32[1,64,4,128]{3,1,2,0:T(8,128)S(1)}, f32[1,64,4,128]{3,1,2,0:T(8,128)S(1)}, u32[]{:S(2)}, u32[]{:S(2)}) collective-permute-start(f32[1,64,4,128]{3,1,2,0:T(8,128)S(1)} %get-tuple-element.14), channel_id=1, source_target_pairs={{1,0},{2,1},{3,2},{4,3},{5,4},{6,5},{7,6},{8,7},{9,8},{10,9},{11,1... | collective-permute-start | bytes 393224 | tf_op jit(solution)/shard_map/ppermute | solution.py:19
  183.0 15.5 %collective-permute-start.26 = (f32[1,64,4,128]{3,1,2,0:T(8,128)S(1)}, f32[1,64,4,128]{3,1,2,0:T(8,128)S(1)}, u32[]{:S(2)}, u32[]{:S(2)}) collective-permute-start(f32[1,64,4,128]{3,1,2,0:T(8,128)S(1)} %get-tuple-element.15), channel_id=1, source_target_pairs={{0,1},{1,2},{2,3},{3,4},{4,5},{5,6},{6,7},{7,8},{8,9},{9,10},{10,1... | collective-permute-start | bytes 393224 | tf_op jit(solution)/shard_map/ppermute | solution.py:16
  188.5 9.4 %collective-permute-start.25 = (f32[1,64,4,128]{3,1,2,0:T(8,128)S(1)}, f32[1,64,4,128]{3,1,2,0:T(8,128)S(1)}, u32[]{:S(2)}, u32[]{:S(2)}) collective-permute-start(f32[1,64,4,128]{3,1,2,0:T(8,128)S(1)} %get-tuple-element.16), channel_id=1, source_target_pairs={{32,0},{64,32},{96,64},{128,96},{160,128},{192,160},{224,192},{256... | collective-permute-start | bytes 393224 | tf_op jit(solution)/shard_map/ppermute | solution.py:19
  213.9 17.0 %collective-permute-start.28 = (f32[1,64,4,128]{3,1,2,0:T(8,128)S(1)}, f32[1,64,4,128]{3,1,2,0:T(8,128)S(1)}, u32[]{:S(2)}, u32[]{:S(2)}) collective-permute-start(f32[1,64,4,128]{3,1,2,0:T(8,128)S(1)} %get-tuple-element.13), channel_id=1, source_target_pairs={{0,32},{32,64},{64,96},{96,128},{128,160},{160,192},{192,224},{224... | collective-permute-start | bytes 393224 | tf_op jit(solution)/shard_map/ppermute | solution.py:16
  221.6 16.2 %collective-permute-start.31 = (f32[1,64,4,128]{3,1,2,0:T(8,128)S(1)}, f32[1,64,4,128]{3,1,2,0:T(8,128)S(1)}, u32[]{:S(2)}, u32[]{:S(2)}) collective-permute-start(f32[1,64,4,128]{3,1,2,0:T(8,128)S(1)} %get-tuple-element.10), channel_id=1, source_target_pairs={{1,0},{2,1},{3,2},{4,3},{5,4},{6,5},{7,6},{8,7},{9,8},{10,9},{11,1... | collective-permute-start | bytes 393224 | tf_op jit(solution)/shard_map/ppermute | solution.py:19
  223.5 13.6 %collective-permute-start.30 = (f32[1,64,4,128]{3,1,2,0:T(8,128)S(1)}, f32[1,64,4,128]{3,1,2,0:T(8,128)S(1)}, u32[]{:S(2)}, u32[]{:S(2)}) collective-permute-start(f32[1,64,4,128]{3,1,2,0:T(8,128)S(1)} %get-tuple-element.11), channel_id=1, source_target_pairs={{0,1},{1,2},{2,3},{3,4},{4,5},{5,6},{6,7},{7,8},{8,9},{9,10},{10,1... | collective-permute-start | bytes 393224 | tf_op jit(solution)/shard_map/ppermute | solution.py:16
  229.0 7.5 %collective-permute-start.29 = (f32[1,64,4,128]{3,1,2,0:T(8,128)S(1)}, f32[1,64,4,128]{3,1,2,0:T(8,128)S(1)}, u32[]{:S(2)}, u32[]{:S(2)}) collective-permute-start(f32[1,64,4,128]{3,1,2,0:T(8,128)S(1)} %get-tuple-element.12), channel_id=1, source_target_pairs={{32,0},{64,32},{96,64},{128,96},{160,128},{192,160},{224,192},{256... | collective-permute-start | bytes 393224 | tf_op jit(solution)/shard_map/ppermute | solution.py:19
  252.6 18.1 %collective-permute-start.35 = (f32[1,64,4,128]{3,1,2,0:T(8,128)S(1)}, f32[1,64,4,128]{3,1,2,0:T(8,128)S(1)}, u32[]{:S(2)}, u32[]{:S(2)}) collective-permute-start(f32[1,64,4,128]{3,1,2,0:T(8,128)S(1)} %get-tuple-element.6), channel_id=1, source_target_pairs={{1,0},{2,1},{3,2},{4,3},{5,4},{6,5},{7,6},{8,7},{9,8},{10,9},{11,1... | collective-permute-start | bytes 393224 | tf_op jit(solution)/shard_map/ppermute | solution.py:19
  254.5 15.5 %collective-permute-start.34 = (f32[1,64,4,128]{3,1,2,0:T(8,128)S(1)}, f32[1,64,4,128]{3,1,2,0:T(8,128)S(1)}, u32[]{:S(2)}, u32[]{:S(2)}) collective-permute-start(f32[1,64,4,128]{3,1,2,0:T(8,128)S(1)} %get-tuple-element.7), channel_id=1, source_target_pairs={{0,1},{1,2},{2,3},{3,4},{4,5},{5,6},{6,7},{7,8},{8,9},{9,10},{10,1... | collective-permute-start | bytes 393224 | tf_op jit(solution)/shard_map/ppermute | solution.py:16
  260.0 9.4 %collective-permute-start.33 = (f32[1,64,4,128]{3,1,2,0:T(8,128)S(1)}, f32[1,64,4,128]{3,1,2,0:T(8,128)S(1)}, u32[]{:S(2)}, u32[]{:S(2)}) collective-permute-start(f32[1,64,4,128]{3,1,2,0:T(8,128)S(1)} %get-tuple-element.8), channel_id=1, source_target_pairs={{32,0},{64,32},{96,64},{128,96},{160,128},{192,160},{224,192},{256... | collective-permute-start | bytes 393224 | tf_op jit(solution)/shard_map/ppermute | solution.py:19
  (29 other events, 189.2 us)
where the time goes:
time: 284 us; the launch traced here: 281 us
  starting transfers between devices  128 us (45%)
  local copies, waits for them, and re-layouts  78.8 us (28%)
  other arithmetic  29.5 us (10%)
  matrix products  25.6 us (9%)
  waiting for transfers between devices  17.4 us (6%)
    ppermute x18, starting transfers between devices, extended_2(): lax.ppermute(lax.slice_in_dim(block, block.shape[dim] - width, None, axis...  89.7 us
    ppermute x18, starting transfers between devices, extended_2(): lax.ppermute(lax.slice_in_dim(block, 0, width, axis=dim), axis, backward)  38.4 us
    unnamed x82, local copies, waits for them, and re-layouts  28.1 us
    dot_general x7, matrix products, block_product(): jnp.einsum('rkij,vrkj->vri', fine_matrix.astype(jnp.float32), picked, pre...  22.8 us
    gather x7, local copies, waits for them, and re-layouts, fine_apply(): jnp.take(extended, flat_cols, axis=1)  22.7 us
    ppermute x18, waiting for transfers between devices, extended_2(): lax.ppermute(lax.slice_in_dim(block, 0, width, axis=dim), axis, backward)  17.2 us
    gather x7, local copies, waits for them, and re-layouts, receive(): jnp.take(blocks, lists, axis=1)  15.1 us
    select_n x8, other arithmetic, fine_apply(): jnp.take(extended, flat_cols, axis=1)  14 us
  transfers between devices with their start and end apart: 36, of which 4 were waited for; matrix products, arithmetic and copies ran while one was open for 11% of the time, Pallas kernels for 0%

commit v1 on v0

v1 whole, which is shorter than its diff:
```python
import functools

import jax
import jax.numpy as jnp
from jax import lax
from jax.experimental import pallas as pl
from jax.experimental.pallas import tpu as pltpu
from jax.sharding import PartitionSpec as P

GROUPS = 2

CENTER = 1.1
RADIUS = 0.9
MESH = pl.DeviceIdType.MESH
F32 = jnp.float32
BF16 = jnp.bfloat16
NT = (((1,), (1,)), ((), ()))
NN = (((1,), (0,)), ((), ()))


def coefficients():
    old = RADIUS / CENTER
    pairs = [(0.0, 1.0 / CENTER)]
    for _ in range(2):
        now = 1.0 / (2.0 * CENTER / RADIUS - old)
        pairs.append((now * old, 2.0 * now / RADIUS))
        old = now
    return pairs


def split(value):
    lead = value.astype(BF16).astype(F32)
    return jnp.concatenate([lead, value - lead], axis=0).astype(BF16)


def fold(value):
    half = value.shape[0] // 2
    return value[:half] + value[half:]


def kernel(
    n_span, n_stream, groups, coef,
    cols, lists, x0_hbm, rhs_hbm, mat_hbm, agg_hbm, cmat_hbm,
    sol_hbm, cor_hbm,
    p_ref, r_ref, x_ref, mat, agg, cmat, dinv, cinv, xa, xb, send, recv,
    asend, arecv, own_hot, halo_hot, cweight, csend, crecv, cres, cout,
    mat_t, in_sem, out_sem, ssem, rsem, asem_s, asem_r,
):
    nv, rows = r_ref.shape
    vg = nv // groups
    rb, nnz, bs, _ = mat.shape
    hb = send.shape[3]
    span, stream = lax.axis_index("span"), lax.axis_index("stream")
    has = (span > 0, span < n_span - 1, stream > 0, stream < n_stream - 1)
    near = ((span - 1, stream), (span + 1, stream), (span, stream - 1), (span, stream + 1))
    order = (2, 3, 0, 1)

    loads = [
        pltpu.make_async_copy(x0_hbm, x_ref, in_sem.at[0]),
        pltpu.make_async_copy(agg_hbm, agg, in_sem.at[1]),
        pltpu.make_async_copy(mat_hbm, mat, in_sem.at[2]),
        pltpu.make_async_copy(rhs_hbm, r_ref, in_sem.at[3]),
        pltpu.make_async_copy(cmat_hbm, cmat, in_sem.at[4]),
    ]
    for one in loads:
        one.start()

    barrier = pltpu.get_barrier_semaphore()
    for d in range(4):
        @pl.when(has[d])
        def _():
            pl.semaphore_signal(barrier, inc=1, device_id=near[d], device_id_type=MESH)

    for d in range(4):
        @pl.when(jnp.logical_not(has[d]))
        def _():
            recv[:, :, d] = jnp.zeros(recv.shape[:2] + recv.shape[3:], F32)
            crecv[:, :, d] = jnp.zeros(crecv.shape[:2] + crecv.shape[3:], F32)
            arecv[d] = jnp.zeros(arecv.shape[1:], jnp.int32)

    peers = sum(one.astype(jnp.int32) for one in has)
    pl.semaphore_wait(barrier, peers)

    def fine_copy(n, g, d):
        return pltpu.make_async_remote_copy(
            src_ref=send.at[n, g, d], dst_ref=recv.at[n, g, d ^ 1],
            send_sem=ssem.at[n, g, d], recv_sem=rsem.at[n, g, d ^ 1],
            device_id=near[d], device_id_type=MESH)

    def coarse_copy(m, g, d):
        return pltpu.make_async_remote_copy(
            src_ref=csend.at[m, g], dst_ref=crecv.at[m, g, d ^ 1],
            send_sem=ssem.at[6 + m, g, d], recv_sem=rsem.at[6 + m, g, d ^ 1],
            device_id=near[d], device_id_type=MESH)

    def agg_copy(d):
        return pltpu.make_async_remote_copy(
            src_ref=asend.at[d], dst_ref=arecv.at[d ^ 1],
            send_sem=asem_s.at[d], recv_sem=asem_r.at[d ^ 1],
            device_id=near[d], device_id_type=MESH)

    def block_of(g, b):
        return (pl.ds(pl.multiple_of(g * vg, vg), vg), pl.ds(b * bs, bs))

    def send_fine(n, g):
        for d in order:
            @pl.when(has[d])
            def _():
                for h in range(hb):
                    send[n, g, d, h] = p_ref[g, lists[0, d * hb + h]]
                fine_copy(n, g, d).start()

    def send_coarse(m, g, value):
        csend[m, g] = value
        for d in order:
            @pl.when(has[d])
            def _():
                coarse_copy(m, g, d).start()

    def arrived(copy_of, first, g):
        for d in order:
            @pl.when(has[d])
            def _():
                copy_of(first, g, d ^ 1).wait_recv()

    def loop(body):
        lax.fori_loop(0, groups, lambda g, _: (body(g), 0)[1], 0)

    loads[0].wait()

    def start(g):
        for b in range(rb):
            value = x_ref[block_of(g, b)]
            p_ref[g, b] = value
            xa[g, b] = split(value)
        send_fine(0, g)

    loop(start)
    loads[1].wait()
    for d in range(4):
        for h in range(hb):
            asend[d, h] = agg[lists[0, d * hb + h]]
    for d in range(4):
        @pl.when(has[d])
        def _():
            agg_copy(d).start()

    row_id = lax.broadcasted_iota(jnp.int32, (bs, bs), 0)
    lane_id = lax.broadcasted_iota(jnp.int32, (bs, bs), 1)
    eye = row_id == lane_id
    for b in range(rb):
        own_hot[:, pl.ds(b * bs, bs)] = (
            jnp.broadcast_to(agg[b], (bs, bs)) == row_id).astype(F32).astype(BF16)
    loads[2].wait()
    for b in range(rb):
        diag = jnp.sum(jnp.where(eye, mat[b, 0].astype(F32), 0.0), axis=0, keepdims=True)
        dinv[pl.ds(b, 1), :] = 1.0 / diag
        for k in range(nnz):
            mat_t[b, pl.ds(k * bs, bs), :] = mat[b, k].T
    loads[4].wait()
    cinv[...] = jnp.broadcast_to(
        1.0 / jnp.sum(jnp.where(eye, cmat[0, 0], 0.0), axis=0, keepdims=True), cinv.shape)
    for k in range(5):
        cweight[k] = split(cmat[0, k])
    for d in range(4):
        @pl.when(has[d])
        def _():
            agg_copy(d ^ 1).wait_recv()
        for h in range(hb):
            halo_hot[d, :, pl.ds(h * bs, bs)] = (
                jnp.broadcast_to(arecv[d, h], (bs, bs)) == row_id
            ).astype(F32).astype(BF16)
    loads[3].wait()

    def take_halo(n, g, x):
        arrived(fine_copy, n, g)
        for d in range(4):
            for h in range(hb):
                x[g, rb + d * hb + h] = split(recv[n, g, d, h])

    def apply(g, x, nxt, alpha, beta, kind):
        for b in range(rb):
            left = jnp.concatenate(
                [x[g, b]] + [x[g, cols[k, b]] for k in range(1, nnz)], axis=1)
            prod = fold(lax.dot_general(left, mat_t[b], NN, preferred_element_type=F32))
            at = block_of(g, b)
            y = p_ref[g, b]
            res = r_ref[at] - prod
            step = beta * (dinv[pl.ds(b, 1), :] * res)
            if alpha:
                step = alpha * y + step
            if kind == "last":
                x_ref[at] = x_ref[at] + y + step
                continue
            if kind != "first":
                x_ref[at] = x_ref[at] + y
            r_ref[at] = res
            if kind != "leftover":
                p_ref[g, b] = step
                nxt[g, b] = split(step)

    def sweep(n, x, nxt, kind):
        def one(g):
            take_halo(n, g, x)
            apply(g, x, nxt, *coef[n % 3], kind)
            send_fine(n + 1, g)

        loop(one)

    sweep(0, xa, xb, "first")
    sweep(1, xb, xa, "")
    sweep(2, xa, xb, "")

    def restrict(g):
        take_halo(3, g, xb)
        apply(g, xb, None, *coef[0], "leftover")
        left = split(r_ref[pl.ds(pl.multiple_of(g * vg, vg), vg), :])
        res = fold(lax.dot_general(left, own_hot[...], NT, preferred_element_type=F32))
        cres[g] = res
        start = cinv[pl.ds(0, 1), :] * res * coef[0][1]
        cout[g] = start
        send_coarse(0, g, start)

    loop(restrict)

    def coarse_sweep(m):
        def one(g):
            arrived(coarse_copy, m, g)
            old = csend[m, g]
            left = jnp.concatenate(
                [split(old)] + [split(crecv[m, g, d]) for d in range(4)], axis=1)
            right = jnp.concatenate([cweight[k] for k in range(5)], axis=1)
            full = fold(lax.dot_general(left, right, NT, preferred_element_type=F32))
            res = cres[g] - (full[:, :bs] + full[:, bs:])
            cres[g] = res
            alpha, beta = coef[m + 1]
            step = alpha * old + beta * (cinv[pl.ds(0, 1), :] * res)
            cout[g] = cout[g] + step
            send_coarse(m + 1, g, step)

        loop(one)

    coarse_sweep(0)
    coarse_sweep(1)
    cor_copy = pltpu.make_async_copy(cout, cor_hbm, out_sem.at[groups])
    cor_copy.start()

    def prolong(g):
        arrived(coarse_copy, 2, g)
        left = split(cout[g])
        for b in range(rb):
            part = lax.dot_general(
                left, own_hot[:, pl.ds(b * bs, bs)], NN, preferred_element_type=F32)
            value = fold(part)
            p_ref[g, b] = value
            xa[g, b] = split(value)
        for d in range(4):
            other = crecv[0, g, d] + crecv[1, g, d] + crecv[2, g, d]
            left = split(other)
            for h in range(hb):
                got = lax.dot_general(
                    left, halo_hot[d, :, pl.ds(h * bs, bs)], NN, preferred_element_type=F32)
                xa[g, rb + d * hb + h] = split(fold(got))

    def coarse_back(g):
        prolong(g)
        apply(g, xa, xb, *coef[0], "")
        send_fine(4, g)

    loop(coarse_back)
    sweep(4, xb, xa, "")

    def out_copy(g):
        at = pl.ds(pl.multiple_of(g * vg, vg), vg)
        return pltpu.make_async_copy(x_ref.at[at], sol_hbm.at[at], out_sem.at[g])

    def finish(g):
        take_halo(5, g, xa)
        apply(g, xa, None, *coef[2], "last")
        out_copy(g).start()

    loop(finish)

    for d in range(4):
        @pl.when(has[d])
        def _():
            def drain(g):
                for n in range(6):
                    fine_copy(n, g, d).wait_send()
                for m in range(3):
                    coarse_copy(m, g, d).wait_send()

            loop(drain)
            agg_copy(d).wait_send()
    loop(lambda g: out_copy(g).wait())
    cor_copy.wait()


def local(
    right_side, start_guess, fine_matrix, fine_columns, send_lists, aggregates, coarse_matrix,
    n_span, n_stream,
):
    nv, rows = right_side.shape
    rb, nnz, bs, _ = fine_matrix.shape
    hb = send_lists.shape[1] // 4
    groups = GROUPS
    vg = nv // groups
    any_spec = pl.BlockSpec(memory_space=pl.ANY)
    smem = pl.BlockSpec(memory_space=pltpu.SMEM)
    dma = pltpu.SemaphoreType.DMA
    solution, correction = pl.pallas_call(
        functools.partial(kernel, n_span, n_stream, groups, coefficients()),
        out_shape=(
            jax.ShapeDtypeStruct((nv, rows), F32),
            jax.ShapeDtypeStruct((groups, vg, bs), F32),
        ),
        in_specs=[smem, smem] + [any_spec] * 5,
        out_specs=(any_spec, any_spec),
        scratch_shapes=[
            pltpu.VMEM((groups, rb, vg, bs), F32),
            pltpu.VMEM((nv, rows), F32),
            pltpu.VMEM((nv, rows), F32),
            pltpu.VMEM((rb, nnz, bs, bs), BF16),
            pltpu.VMEM((rb, 1, bs), jnp.int32),
            pltpu.VMEM((1, 5, bs, bs), F32),
            pltpu.VMEM((rb, bs), F32),
            pltpu.VMEM((8, bs), F32),
            pltpu.VMEM((groups, rb + 4 * hb, 2 * vg, bs), BF16),
            pltpu.VMEM((groups, rb + 4 * hb, 2 * vg, bs), BF16),
            pltpu.VMEM((6, groups, 4, hb, vg, bs), F32),
            pltpu.VMEM((6, groups, 4, hb, vg, bs), F32),
            pltpu.VMEM((4, hb, 1, bs), jnp.int32),
            pltpu.VMEM((4, hb, 1, bs), jnp.int32),
            pltpu.VMEM((bs, rows), BF16),
            pltpu.VMEM((4, bs, hb * bs), BF16),
            pltpu.VMEM((5, 2 * bs, bs), BF16),
            pltpu.VMEM((3, groups, vg, bs), F32),
            pltpu.VMEM((3, groups, 4, vg, bs), F32),
            pltpu.VMEM((groups, vg, bs), F32),
            pltpu.VMEM((groups, vg, bs), F32),
            pltpu.VMEM((rb, nnz * bs, bs), BF16),
            dma((5,)),
            dma((groups + 1,)),
            dma((9, groups, 4)),
            dma((9, groups, 4)),
            dma((4,)),
            dma((4,)),
        ],
        compiler_params=pltpu.CompilerParams(
            collective_id=0, has_side_effects=True, vmem_limit_bytes=62 * 1024 * 1024),
        name="cycle",
    )(
        fine_columns.T, send_lists, start_guess, right_side, fine_matrix,
        aggregates.reshape(rb, 1, bs), coarse_matrix,
    )
    return solution, correction.reshape(nv, bs)


def solution(mesh):
    placed = (
        P(None, ("span", "stream")),
        P(None, ("span", "stream")),
        P(("span", "stream"), None, None, None),
        P(("span", "stream"), None),
        P(("span", "stream"), None),
        P(("span", "stream")),
        P(("span", "stream"), None, None, None),
    )
    return jax.shard_map(
        functools.partial(local, n_span=mesh.shape["span"], n_stream=mesh.shape["stream"]),
        mesh=mesh,
        in_specs=placed,
        out_specs=(P(None, ("span", "stream")), P(None, ("span", "stream"))),
        check_vma=False,
    )
```

time: 284 us -> 60.6 us (0.21)
  the two profiles are of different devices: /device:TPU:251 before, /device:TPU:135 now
where the time goes in v1:
time: 60.6 us; the launch traced here: 60.3 us
  Pallas kernels  56.4 us (93%)
  local copies, waits for them, and re-layouts  3.25 us (5%)
  between operations  0.64 us (1%)
    pallas_call x1, Pallas kernels, local(): pl.pallas_call(functools.partial(kernel, n_span, n_stream, groups, coeffi...  56.4 us
    unnamed x2, local copies, waits for them, and re-layouts  3.25 us

profile of v1, /device:TPU:135, one launch (start us, length us, event | category | flops | bytes accessed | tf_op | source)
XLA Modules:
  0.0 60.3 jit_solution(3997278733555589080)
XLA Ops:
  0.6 56.4 %cycle.1 = (f32[64,2048]{1,0:T(8,128)}, f32[2,32,128]{2,1,0:T(8,128)}) custom-call(s32[5,16]{1,0:T(8,128)} %bitcast.5, s32[1,16]{1,0:T(1,128)} %lists.1, f32[64,2048]{1,0:T(8,128)} %x0_hbm.1, f32[64,2048]{1,0:T(8,128)} %rhs_hbm.1, bf16[16,5,128,128]{3,2,1,0:T(8,128)(2,1)} %mat_hbm.1, s32[16,1,128]{2,1,0:T(1,128)} %bitcast.4, f32[1,5,128,128]{3,2,1,0:T(8,128)} %cmat_hbm.1), custom_call_target="tpu_custom_call" | custom-call | tf_op jit(solution)/shard_map/cycle/pallas_call | solution.py:311
  57.1 1.9 %copy.11 = f32[64,2048]{1,0:T(8,128)} copy(f32[64,2048]{1,0:T(8,128)} %get-tuple-element.8) | data formatting | bytes 1048576
  58.9 1.4 %copy.12 = f32[64,128]{1,0:T(8,128)} copy(f32[64,128]{1,0:T(8,128)} %bitcast.3) | data formatting | bytes 65536
